TPU v7x, 32 devices: a whole 2x2x4 slice. The times are simulated.
32 devices in a mesh: rep: 4 (over x, core), fsdp: 8 (over z, y).
Axes of the slice: x: 2, y: 2, z: 4, core: 2. Of those that a mesh axis runs over, the one named last changes fastest.
Arguments:
- tokens: bfloat16 [2, 18432, 1024], P(None, ('rep', 'fsdp')), may hold values from -6 to 6
- out_grad: bfloat16 [2, 18432, 1024], P(None, ('rep', 'fsdp')), may hold values from -6 to 6
- image_starts: int32 [2, 4, 6], P(None, 'rep'), may hold values from 0 to 4031, as said below
- first_gain: bfloat16 [1024], P('fsdp'), may hold values from 0.5 to 1.5
- first_shift: bfloat16 [1024], P('fsdp'), may hold values from -1.5 to 1.5
- qkv_weight: bfloat16 [1024, 3072], P('fsdp'), may hold values from -0.1875 to 0.1875
- query_bias: bfloat16 [1024], P('fsdp'), may hold values from -1.5 to 1.5
- value_bias: bfloat16 [1024], P('fsdp'), may hold values from -1.5 to 1.5
- out_weight: bfloat16 [1024, 1024], P('fsdp'), may hold values from -1 to 1
- out_bias: bfloat16 [1024], P('fsdp'), may hold values from -1.5 to 1.5
- second_gain: bfloat16 [1024], P('fsdp'), may hold values from 0.5 to 1.5
- second_shift: bfloat16 [1024], P('fsdp'), may hold values from -1.5 to 1.5
- up_weight: bfloat16 [1024, 4096], P('fsdp'), may hold values from -0.1875 to 0.1875
- up_bias: bfloat16 [4096], P('fsdp'), may hold values from -1.5 to 1.5
- down_weight: bfloat16 [4096, 1024], P('fsdp'), may hold values from -0.09375 to 0.09375
- down_bias: bfloat16 [1024], P('fsdp'), may hold values from -1.5 to 1.5
Outputs:
- layer_out: bfloat16 [2, 18432, 1024], P(None, ('rep', 'fsdp'))
- tokens_grad: bfloat16 [2, 18432, 1024], P(None, ('rep', 'fsdp'))
- first_gain_grad: float32 [1024], P('fsdp')
- first_shift_grad: float32 [1024], P('fsdp')
- qkv_weight_grad: float32 [1024, 3072], P('fsdp')
- query_bias_grad: float32 [1024], P('fsdp')
- value_bias_grad: float32 [1024], P('fsdp')
- out_weight_grad: float32 [1024, 1024], P('fsdp')
- out_bias_grad: float32 [1024], P('fsdp')
- second_gain_grad: float32 [1024], P('fsdp')
- second_shift_grad: float32 [1024], P('fsdp')
- up_weight_grad: float32 [1024, 4096], P('fsdp')
- up_bias_grad: float32 [4096], P('fsdp')
- down_weight_grad: float32 [4096, 1024], P('fsdp')
- down_bias_grad: float32 [1024], P('fsdp')
Inputs may be any that keep to these rules, and one draw needn't show every extreme that they name: `image_starts`: for each micro-batch and replica group, 6 image starts in rising order within the group's 8 * 576 packed positions; each image's 577 tokens end at or before the next image's start and within the group's positions. The first image starts at 0 and the last ends at the last position; positions in no image are padding.
All inputs are finite; a program needn't handle non-finite values.
Results may differ from a plain program's by a relative error of at most 0.015.
Values may be sent and summed in bfloat16 or wider, within the bound.
A program may use at most 320 MiB of HBM per device.

v0:
```python
from functools import partial

import jax
import jax.numpy as jnp
from jax import lax
from jax.sharding import PartitionSpec as P

D = 1024
H = 16
HD = 64
IMG = 577


epsilon = 1e-06
masked_score = -1e30


def extended(block, sides, width):
    for axis, dim in sides:
        count = lax.axis_size(axis)
        forward = [(i, i + 1) for i in range(count - 1)]
        backward = [(target, source) for source, target in forward]
        low = lax.ppermute(
            lax.slice_in_dim(block, block.shape[dim] - width, None, axis=dim), axis, forward
        )
        high = lax.ppermute(lax.slice_in_dim(block, 0, width, axis=dim), axis, backward)
        block = jnp.concatenate([low, block, high], axis=dim)
    return block


def shortened(value):

    def short(part):
        return part.astype(jnp.bfloat16) if part.dtype == jnp.float32 else part

    return jax.tree.map(short, value)


def product(left, right):
    return jnp.dot(left, right, preferred_element_type=jnp.float32)


def product_left(left, right):
    return lax.dot_general(
        left, right, (((0,), (0,)), ((), ())), preferred_element_type=jnp.float32
    )


def product_right(left, right):
    return lax.dot_general(
        left, right, (((1,), (1,)), ((), ())), preferred_element_type=jnp.float32
    )


def norm_stats(values):
    centre = values - jnp.mean(values, axis=-1, keepdims=True)
    spread = jnp.mean(centre * centre, axis=-1, keepdims=True)
    factor = lax.rsqrt(spread + epsilon)
    return (centre * factor, factor)


def norm_back(grad_normed, normed, factor):
    return factor * (
        grad_normed
        - jnp.mean(grad_normed, axis=-1, keepdims=True)
        - normed * jnp.mean(grad_normed * normed, axis=-1, keepdims=True)
    )


def label_rows(places, starts):
    after = starts[None, :] <= places[:, None]
    inside = after & (places[:, None] < starts[None, :] + IMG)
    counted = jnp.sum(after.astype(jnp.int32), axis=1) - 1
    return jnp.where(jnp.any(inside, axis=1), counted, -1)


def allowed(query_start, shard_rows, starts):
    query_place = query_start + jnp.arange(shard_rows, dtype=jnp.int32)
    key_place = query_start - shard_rows + jnp.arange(3 * shard_rows, dtype=jnp.int32)
    query_label = label_rows(query_place, starts)
    key_label = label_rows(key_place, starts)
    same_image = (query_label[:, None] == key_label[None, :]) & (query_label[:, None] >= 0)
    return same_image | (query_place[:, None] == key_place[None, :])


def split_heads(values):
    return values.reshape(values.shape[0], H, HD).transpose(1, 0, 2)


def join_heads(values):
    return values.transpose(1, 0, 2).reshape(values.shape[1], H * HD)


def heads_forward(query_heads, key_heads, value_heads, permit):
    score_scale = HD ** (-0.5)

    def one_head(operands):
        query_one, key_one, value_one = operands
        scores = jnp.where(permit, product_right(query_one, key_one) * score_scale, masked_score)
        largest = jnp.max(scores, axis=-1, keepdims=True)
        raised = jnp.exp(scores - largest)
        row_total = jnp.sum(raised, axis=-1, keepdims=True)
        attention = (raised / row_total).astype(jnp.bfloat16)
        return (product(attention, value_one), (largest + jnp.log(row_total))[:, 0])

    return lax.map(one_head, (query_heads, key_heads, value_heads))


def heads_backward(query_heads, key_heads, value_heads, log_totals, grad_heads, permit):
    score_scale = HD ** (-0.5)

    def one_head(operands):
        query_one, key_one, value_one, log_one, grad_one = operands
        scores = jnp.where(permit, product_right(query_one, key_one) * score_scale, masked_score)
        attention = jnp.exp(scores - log_one[:, None])
        grad_probs = product_right(grad_one, value_one)
        row_inner = jnp.sum(attention * grad_probs, axis=-1, keepdims=True)
        grad_scores = (attention * (grad_probs - row_inner)).astype(jnp.bfloat16)
        grad_query = product(grad_scores, key_one) * score_scale
        grad_key = product_left(grad_scores, query_one) * score_scale
        grad_value = product_left(attention.astype(jnp.bfloat16), grad_one)
        return (grad_query, grad_key, grad_value)

    return lax.map(one_head, (query_heads, key_heads, value_heads, log_totals, grad_heads))


def forward(tokens_one, starts, weights, query_start):
    (
        first_gain,
        first_shift,
        qkv_weight,
        query_bias,
        value_bias,
        out_weight,
        out_bias,
        second_gain,
        second_shift,
        up_weight,
        up_bias,
        down_weight,
        down_bias,
    ) = weights
    shard_rows = tokens_one.shape[0]
    inputs = tokens_one.astype(jnp.float32)
    normed_one, factor_one = norm_stats(inputs)
    first_in = (
        normed_one * first_gain.astype(jnp.float32) + first_shift.astype(jnp.float32)
    ).astype(jnp.bfloat16)
    joined = product(first_in, qkv_weight)
    queries = (joined[:, :D] + query_bias.astype(jnp.float32)).astype(jnp.bfloat16)
    key_value = jnp.concatenate(
        [joined[:, D : 2 * D], joined[:, 2 * D :] + value_bias.astype(jnp.float32)], axis=1
    ).astype(jnp.bfloat16)
    window = extended(key_value, (("fsdp", 0),), shard_rows)
    permit = allowed(query_start, shard_rows, starts)
    query_heads = split_heads(queries)
    key_heads = split_heads(window[:, :D])
    value_heads = split_heads(window[:, D:])
    mixed_heads, log_totals = heads_forward(query_heads, key_heads, value_heads, permit)
    mixed_rows = join_heads(mixed_heads).astype(jnp.bfloat16)
    middle = inputs + product(mixed_rows, out_weight) + out_bias.astype(jnp.float32)
    normed_two, factor_two = norm_stats(middle)
    second_in = (
        normed_two * second_gain.astype(jnp.float32) + second_shift.astype(jnp.float32)
    ).astype(jnp.bfloat16)
    hidden = product(second_in, up_weight) + up_bias.astype(jnp.float32)
    active = jax.nn.gelu(hidden, approximate=False).astype(jnp.bfloat16)
    layer_out = (middle + product(active, down_weight) + down_bias.astype(jnp.float32)).astype(
        jnp.bfloat16
    )
    saved_state = (
        normed_one,
        factor_one,
        first_in,
        query_heads,
        key_heads,
        value_heads,
        log_totals,
        permit,
        mixed_rows,
        normed_two,
        factor_two,
        second_in,
        hidden,
        active,
    )
    return (layer_out, saved_state)


def backward(cotangent, weights, saved_state):
    (
        first_gain,
        first_shift,
        qkv_weight,
        query_bias,
        value_bias,
        out_weight,
        out_bias,
        second_gain,
        second_shift,
        up_weight,
        up_bias,
        down_weight,
        down_bias,
    ) = weights
    (
        normed_one,
        factor_one,
        first_in,
        query_heads,
        key_heads,
        value_heads,
        log_totals,
        permit,
        mixed_rows,
        normed_two,
        factor_two,
        second_in,
        hidden,
        active,
    ) = saved_state
    shard_rows = cotangent.shape[0]
    grad_out = cotangent.astype(jnp.float32)
    down_grad = product_left(active, cotangent)
    down_bias_grad = jnp.sum(grad_out, axis=0)
    grad_active = product_right(cotangent, down_weight)
    gelu_pull = jax.vjp(partial(jax.nn.gelu, approximate=False), hidden)[1]
    grad_hidden = gelu_pull(grad_active)[0].astype(jnp.bfloat16)
    up_grad = product_left(second_in, grad_hidden)
    up_bias_grad = jnp.sum(grad_hidden.astype(jnp.float32), axis=0)
    grad_second = product_right(grad_hidden, up_weight)
    second_gain_grad = jnp.sum(grad_second * normed_two, axis=0)
    second_shift_grad = jnp.sum(grad_second, axis=0)
    grad_middle = grad_out + norm_back(
        grad_second * second_gain.astype(jnp.float32), normed_two, factor_two
    )
    grad_branch = grad_middle.astype(jnp.bfloat16)
    out_weight_grad = product_left(mixed_rows, grad_branch)
    out_bias_grad = jnp.sum(grad_branch.astype(jnp.float32), axis=0)
    grad_mixed = product_right(grad_branch, out_weight).astype(jnp.bfloat16)
    grad_query, grad_key, grad_value = heads_backward(
        query_heads, key_heads, value_heads, log_totals, split_heads(grad_mixed), permit
    )
    grad_window = jnp.concatenate([join_heads(grad_key), join_heads(grad_value)], axis=1)
    rim_rows = jnp.concatenate([grad_window[:shard_rows], grad_window[2 * shard_rows :]], axis=0)
    returned = extended(rim_rows.astype(jnp.bfloat16), (("fsdp", 0),), shard_rows).astype(
        rim_rows.dtype
    )
    grad_pair = (
        grad_window[shard_rows : 2 * shard_rows]
        + returned[:shard_rows]
        + returned[3 * shard_rows :]
    )
    grad_joined = jnp.concatenate([join_heads(grad_query), grad_pair], axis=1).astype(jnp.bfloat16)
    qkv_grad = product_left(first_in, grad_joined)
    joined_sums = jnp.sum(grad_joined.astype(jnp.float32), axis=0)
    query_bias_grad = joined_sums[:D]
    value_bias_grad = joined_sums[2 * D :]
    grad_first = product_right(grad_joined, qkv_weight)
    first_gain_grad = jnp.sum(grad_first * normed_one, axis=0)
    first_shift_grad = jnp.sum(grad_first, axis=0)
    tokens_grad = (
        grad_middle + norm_back(grad_first * first_gain.astype(jnp.float32), normed_one, factor_one)
    ).astype(jnp.bfloat16)
    weight_grads = (
        first_gain_grad,
        first_shift_grad,
        qkv_grad,
        query_bias_grad,
        value_bias_grad,
        out_weight_grad,
        out_bias_grad,
        second_gain_grad,
        second_shift_grad,
        up_grad,
        up_bias_grad,
        down_grad,
        down_bias_grad,
    )
    return (tokens_grad, weight_grads)


def body(
    tokens,
    out_grad,
    image_starts,
    first_gain,
    first_shift,
    qkv_weight,
    query_bias,
    value_bias,
    out_weight,
    out_bias,
    second_gain,
    second_shift,
    up_weight,
    up_bias,
    down_weight,
    down_bias,
):
    shards = (
        first_gain,
        first_shift,
        qkv_weight,
        query_bias,
        value_bias,
        out_weight,
        out_bias,
        second_gain,
        second_shift,
        up_weight,
        up_bias,
        down_weight,
        down_bias,
    )
    micro_count = tokens.shape[0]
    shard_rows = tokens.shape[1]
    query_start = lax.axis_index("fsdp") * shard_rows
    outputs = []
    input_grads = []
    summed = None
    for micro_index in range(micro_count):
        weights = (
            lax.all_gather(shards[0], "fsdp", axis=0, tiled=True),
            lax.all_gather(shards[1], "fsdp", axis=0, tiled=True),
            lax.all_gather(shards[2], "fsdp", axis=0, tiled=True),
            lax.all_gather(shards[3], "fsdp", axis=0, tiled=True),
            lax.all_gather(shards[4], "fsdp", axis=0, tiled=True),
            lax.all_gather(shards[5], "fsdp", axis=0, tiled=True),
            lax.all_gather(shards[6], "fsdp", axis=0, tiled=True),
            lax.all_gather(shards[7], "fsdp", axis=0, tiled=True),
            lax.all_gather(shards[8], "fsdp", axis=0, tiled=True),
            lax.all_gather(shards[9], "fsdp", axis=0, tiled=True),
            lax.all_gather(shards[10], "fsdp", axis=0, tiled=True),
            lax.all_gather(shards[11], "fsdp", axis=0, tiled=True),
            lax.all_gather(shards[12], "fsdp", axis=0, tiled=True),
        )
        layer_out, saved_state = forward(
            tokens[micro_index], image_starts[micro_index, 0], weights, query_start
        )
        weights = (
            lax.all_gather(shards[0], "fsdp", axis=0, tiled=True),
            lax.all_gather(shards[1], "fsdp", axis=0, tiled=True),
            lax.all_gather(shards[2], "fsdp", axis=0, tiled=True),
            lax.all_gather(shards[3], "fsdp", axis=0, tiled=True),
            lax.all_gather(shards[4], "fsdp", axis=0, tiled=True),
            lax.all_gather(shards[5], "fsdp", axis=0, tiled=True),
            lax.all_gather(shards[6], "fsdp", axis=0, tiled=True),
            lax.all_gather(shards[7], "fsdp", axis=0, tiled=True),
            lax.all_gather(shards[8], "fsdp", axis=0, tiled=True),
            lax.all_gather(shards[9], "fsdp", axis=0, tiled=True),
            lax.all_gather(shards[10], "fsdp", axis=0, tiled=True),
            lax.all_gather(shards[11], "fsdp", axis=0, tiled=True),
            lax.all_gather(shards[12], "fsdp", axis=0, tiled=True),
        )
        tokens_grad, weight_grads = backward(out_grad[micro_index], weights, saved_state)
        weight_grads = (
            lax.psum_scatter(weight_grads[0], "fsdp", scatter_dimension=0, tiled=True),
            lax.psum_scatter(weight_grads[1], "fsdp", scatter_dimension=0, tiled=True),
            lax.psum_scatter(weight_grads[2], "fsdp", scatter_dimension=0, tiled=True),
            lax.psum_scatter(weight_grads[3], "fsdp", scatter_dimension=0, tiled=True),
            lax.psum_scatter(weight_grads[4], "fsdp", scatter_dimension=0, tiled=True),
            lax.psum_scatter(weight_grads[5], "fsdp", scatter_dimension=0, tiled=True),
            lax.psum_scatter(weight_grads[6], "fsdp", scatter_dimension=0, tiled=True),
            lax.psum_scatter(weight_grads[7], "fsdp", scatter_dimension=0, tiled=True),
            lax.psum_scatter(weight_grads[8], "fsdp", scatter_dimension=0, tiled=True),
            lax.psum_scatter(weight_grads[9], "fsdp", scatter_dimension=0, tiled=True),
            lax.psum_scatter(weight_grads[10], "fsdp", scatter_dimension=0, tiled=True),
            lax.psum_scatter(weight_grads[11], "fsdp", scatter_dimension=0, tiled=True),
            lax.psum_scatter(weight_grads[12], "fsdp", scatter_dimension=0, tiled=True),
        )
        if summed is None:
            summed = weight_grads
        else:
            summed = jax.tree.map(jnp.add, summed, weight_grads)
        outputs.append(layer_out)
        input_grads.append(tokens_grad)
    totals = jax.tree.map(lambda part: part.astype(jnp.float32), lax.psum(shortened(summed), "rep"))
    return (
        jnp.stack(outputs),
        jnp.stack(input_grads),
        totals[0],
        totals[1],
        totals[2],
        totals[3],
        totals[4],
        totals[5],
        totals[6],
        totals[7],
        totals[8],
        totals[9],
        totals[10],
        totals[11],
        totals[12],
    )


def solution(mesh):
    placed = (
        P(None, ("rep", "fsdp"), None),
        P(None, ("rep", "fsdp"), None),
        P(None, "rep", None),
        P("fsdp"),
        P("fsdp"),
        P("fsdp", None),
        P("fsdp"),
        P("fsdp"),
        P("fsdp", None),
        P("fsdp"),
        P("fsdp"),
        P("fsdp"),
        P("fsdp", None),
        P("fsdp"),
        P("fsdp", None),
        P("fsdp"),
    )
    return jax.shard_map(
        body,
        mesh=mesh,
        in_specs=placed,
        out_specs=(
            P(None, ("rep", "fsdp"), None),
            P(None, ("rep", "fsdp"), None),
            P("fsdp"),
            P("fsdp"),
            P("fsdp", None),
            P("fsdp"),
            P("fsdp"),
            P("fsdp", None),
            P("fsdp"),
            P("fsdp"),
            P("fsdp"),
            P("fsdp", None),
            P("fsdp"),
            P("fsdp", None),
            P("fsdp"),
        ),
        check_vma=False,
    )
```

profile of v0, /device:TPU:0, one launch (start us, length us, event | category | flops | bytes accessed | tf_op | source)
XLA Modules:
  0.0 2277.4 jit_solution(11988545740909782724)
XLA Ops:
  9.5 22.7 all-gather.1
  32.2 17.3 all-gather
  49.5 18.6 all-gather.3
  68.1 17.4 all-gather.2
  88.4 23.4 %all-gather.14.cloned.1.call-done = bf16[1024,3072]{1,0:T(8,128)(2,1)} async-done(((bf16[128,3072]{1,0:T(8,128)(2,1)}), bf16[1024,3072]{1,0:T(8,128)(2,1)}) %all-gather.14.cloned.1.call-update) | async-done | bytes 6291472 | tf_op jit(solution)/shard_map/all_gather | solution.py:326
  135.9 132.0 %all-gather.4 = bf16[8,1,128]{2,1,0:T(2,128)(2,1)S(1)} all-gather(bf16[1,1,128]{2,1,0:T(2,128)(2,1)S(1)} %bitcast.452), channel_id=1, replica_groups=mesh['rep'=4,'fsdp'=8] {'fsdp'}, dimensions={0}, use_global_device_ids=true | all-gather | bytes 2304 | tf_op jit(solution)/shard_map/all_gather | solution.py:330
  268.4 27.4 %all-gather.7 = bf16[8,1,512]{2,1,0:T(2,128)(2,1)S(1)} all-gather(bf16[1,1,512]{2,1,0:T(2,128)(2,1)S(1)} %reshape.313), channel_id=1, replica_groups=mesh['rep'=4,'fsdp'=8] {'fsdp'}, dimensions={0}, use_global_device_ids=true | all-gather | bytes 9216 | tf_op jit(solution)/shard_map/all_gather | solution.py:334
  296.4 16.9 all-gather.6
  313.4 19.0 all-gather.5
  398.5 118.9 %while.57 = (s32[]{:T(128)}, bf16[16,576,64]{1,2,0:T(8,128)(2,1)}, f32[16,576]{1,0:T(8,128)}, bf16[16,576,64]{2,1,0:T(8,128)(2,1)}, bf16[16,1728,64]{2,1,0:T(8,1...) while((s32[]{:T(128)}, bf16[16,576,64]{1,2,0:T(8,128)(2,1)}, ...), condition=%wide.region_21.22_spmd.clone, body=%wide.region_18.21_spmd.clone.sunk | while | flops 266747328 | bytes 13193609 | solution.py:106
  554.9 88.6 %while.56 = (s32[]{:T(128)}, bf16[16,576,64]{1,2,0:T(8,128)(2,1)S(1)}, f32[16,576]{1,0:T(8,128)S(1)}, bf16[16,576,64]{2,1,0:T(8,128)(2,1)}, bf16[16,1728,64]{2,1...) while((s32[]{:T(128)}, ...), condition=%wide.region_9.10_spmd.clone, body=%wide.region_6.9_spmd.clone.sunk | while | flops 266747328 | bytes 13341129 | solution.py:106
  661.6 53.4 %multiply_convert_fusion.3 = (bf16[576,4096]{1,0:T(8,128)(2,1)}, f32[576,4096]{1,0:T(8,128)}, bf16[576,4096]{1,0:T(8,128)(2,1)}, f32[576,4096]{1,0:T(8,128)}, f32[576,4096]{1,0:T(8,128)}) fusion(f32[4096]{0:T(1024)S(1)} %bitcast.431, f32[576,4096]{1,0:T(8,128)S(1)} %fusion.193, bf16[1024,4096]{1,0:T(8,128)(2,1)S(1)} %copy-done.84, ...), kind=kOutput, calls=%fused_computation.131 | convolution fusion | flops 5146214400 | bytes 57963008 | tf_op jit(solution)/shard_map/dot_general | solution.py:40
  714.9 17.0 convert_reduce_fusion
  742.5 17.0 convert_reduce_fusion.1
  759.5 13.3 multiply_reduce_fusion.3
  790.2 185.3 %while.59 = (s32[]{:T(128)}, bf16[16,576,64]{1,2,0:T(8,128)(2,1)S(1)}, f32[16,1728,64]{1,2,0:T(8,128)}, f32[16,1728,64]{1,2,0:T(8,128)}, bf16[16,576,64]{2,1,0:T...) while((s32[]{:T(128)}, ...), condition=%wide.region_35.36_spmd.clone, body=%wide.region_33.35_spmd.clone.sunk | while | flops 650096064 | bytes 32987544 | solution.py:124
  1023.6 209.1 %while.58 = (s32[]{:T(128)}, bf16[16,576,64]{1,2,0:T(8,128)(2,1)}, f32[16,1728,64]{1,2,0:T(8,128)}, f32[16,1728,64]{1,2,0:T(8,128)}, bf16[16,576,64]{2,1,0:T(8,1...) while((s32[]{:T(128)}, bf16[16,576,64]{1,2,0:T(8,128)(2,1)}, ...), condition=%wide.region_28.29_spmd.clone, body=%wide.region_26.28_spmd.clone.sunk | while | flops 650096064 | bytes 32764120 | solution.py:124
  1267.9 15.8 concatenate.48
  1283.7 11.7 convert_element_type.311
  1295.4 44.2 %collective-permute-done.4 = bf16[576,2048]{1,0:T(8,128)(2,1)} collective-permute-done((bf16[576,2048]{1,0:T(8,128)(2,1)}, bf16[576,2048]{1,0:T(8,128)(2,1)}, u32[]{:S(2)}, u32[]{:S(2)}) %collective-permute-start.4) | collective-permute-done | bytes 2359328 | tf_op jit(solution)/shard_map/ppermute | solution.py:23
  1348.3 15.8 concatenate.45
  1405.2 12.4 convolution_add_fusion.2
  1419.3 13.1 fusion.191
  1432.5 15.3 convolution_add_fusion
  1447.8 13.3 fusion.155
  1461.1 15.1 convolution_add_fusion.1
  1476.9 19.5 all-gather.8
  1536.0 88.4 %reduce-scatter.5.cloned.1.call-done = f32[128,3072]{1,0:T(8,128)} async-done(((f32[1024,3072]{1,0:T(8,128)}), f32[128,3072]{1,0:T(8,128)}) %reduce-scatter.5.cloned.1.call-update) | async-done | bytes 1572880 | tf_op jit(solution)/shard_map/reduce_scatter | solution.py:360
  1626.8 280.8 %reduce-scatter.9.cloned.1.call-done = f32[128,4096]{1,0:T(8,128)} async-done(((f32[1024,4096]{1,0:T(8,128)}), f32[128,4096]{1,0:T(8,128)}) %reduce-scatter.9.cloned.1.call-update) | async-done | bytes 2097168 | tf_op jit(solution)/shard_map/reduce_scatter | solution.py:367
  1910.2 280.4 %reduce-scatter.11.cloned.1.call-done = f32[512,1024]{1,0:T(8,128)} async-done(((f32[4096,1024]{1,0:T(8,128)}), f32[512,1024]{1,0:T(8,128)}) %reduce-scatter.11.cloned.1.call-update) | async-done | bytes 2097168 | tf_op jit(solution)/shard_map/reduce_scatter | solution.py:369
  2193.5 35.9 %all-reduce.9 = (bf16[1024]{0:T(1024)(128)(2,1)S(1)}, bf16[1024]{0:T(1024)(128)(2,1)S(1)}, bf16[1024]{0:T(1024)(128)(2,1)S(1)}, bf16[1024]{0:T(1024)(128)(2,1)S(...) all-reduce(f32[1024]{0:T(1024)S(1)} %add.454, ...), channel_id=15, replica_groups=mesh['rep'=4,'fsdp'=8] {'fsdp'}, use_global_device_ids=true, to_apply=%region_39.40.clone | all-reduce | flops 12288 | bytes 73728
  2246.8 15.3 all-reduce.14.cloned.1.call-done
  (782 shorter events, 986.9 us)
Async XLA Ops:
  7.2 80.4 %copy-start.3 = (bf16[2,576,1024]{2,1,0:T(8,128)(2,1)S(1)}, bf16[2,576,1024]{2,1,0:T(8,128)(2,1)}, u32[]{:S(2)}) copy-start(bf16[2,576,1024]{2,1,0:T(8,128)(2,1)} %param.24) | copy-start | bytes 7077892
  7.2 104.6 %all-gather.14.cloned.1.call-start = ((), (), s32[]{:S(2)}) async-start(), calls=%async_computation.4 | async-start | bytes 7077888 | tf_op jit(solution)/shard_map/all_gather | solution.py:326
  7.9 509.4 %all-gather.16.cloned.1.call-start = ((), (), s32[]{:S(2)}) async-start(), calls=%async_computation.5 | async-start | bytes 2359296 | tf_op jit(solution)/shard_map/all_gather | solution.py:329
  8.7 640.3 %all-gather.18.cloned.1.call-start = ((), (), s32[]{:S(2)}) async-start(), calls=%async_computation.6 | async-start | bytes 9437184 | tf_op jit(solution)/shard_map/all_gather | solution.py:333
  9.4 705.5 %all-gather.20.cloned.1.call-start = ((), (), s32[]{:S(2)}) async-start(), calls=%async_computation.7 | async-start | bytes 9437184 | tf_op jit(solution)/shard_map/all_gather | solution.py:335
  32.2 86.1 %copy-start.74 = (f32[8,1,128]{2,1,0:T(1,128)}, f32[8,1,128]{2,1,0:T(1,128)S(1)}, u32[]{:S(2)}) copy-start(f32[8,1,128]{2,1,0:T(1,128)S(1)} %convert_element_type.346) | copy-start | bytes 12292
  49.5 68.8 %copy-start.56 = (f32[8,1,128]{2,1,0:T(1,128)}, f32[8,1,128]{2,1,0:T(1,128)S(1)}, u32[]{:S(2)}) copy-start(f32[8,1,128]{2,1,0:T(1,128)S(1)} %convert_element_type.345) | copy-start | bytes 12292
  87.5 30.8 %copy-start.47 = (f32[576]{0:T(1024)}, f32[576]{0:T(1024)S(1)}, u32[]{:S(2)}) copy-start(f32[576]{0:T(1024)S(1)} %get-tuple-element.757) | copy-start | bytes 6916
  125.9 142.5 %copy-start.78 = (bf16[512]{0:T(512)(128)(2,1)S(1)}, bf16[512]{0:T(512)(128)(2,1)}, u32[]{:S(2)}) copy-start(bf16[512]{0:T(512)(128)(2,1)} %param.37) | copy-start | bytes 3076
  125.9 170.5 %copy-start.82 = (bf16[128]{0:T(256)(128)(2,1)S(1)}, bf16[128]{0:T(256)(128)(2,1)}, u32[]{:S(2)}) copy-start(bf16[128]{0:T(256)(128)(2,1)} %param.35) | copy-start | bytes 772
  125.9 207.1 %copy-start.77 = (s32[2,1,6]{2,1,0:T(1,128)S(1)}, s32[2,1,6]{2,1,0:T(1,128)}, u32[]{:S(2)}) copy-start(s32[2,1,6]{2,1,0:T(1,128)} %param.26) | copy-start | bytes 148
  128.5 232.7 %collective-permute-start.3 = (bf16[576,2048]{1,0:T(8,128)(2,1)}, bf16[576,2048]{1,0:T(8,128)(2,1)}, u32[]{:S(2)}, u32[]{:S(2)}) collective-permute-start(bf16[576,2048]{1,0:T(8,128)(2,1)} %pad_maximum_fusion.7), channel_id=1, source_target_pairs={{1,0},{2,1},{3,2},{4,3},{5,4},{6,5},{7,6},{9,8},{10,9},{11,10},{12... | collective-permute-start | bytes 7077896 | tf_op jit(solution)/shard_map/ppermute | solution.py:26
  129.8 231.4 %collective-permute-start.2 = (bf16[576,2048]{1,0:T(8,128)(2,1)}, bf16[576,2048]{1,0:T(8,128)(2,1)}, u32[]{:S(2)}, u32[]{:S(2)}) collective-permute-start(bf16[576,2048]{1,0:T(8,128)(2,1)} %pad_maximum_fusion.7), channel_id=1, source_target_pairs={{0,1},{1,2},{2,3},{3,4},{4,5},{5,6},{6,7},{8,9},{9,10},{10,11},{11... | collective-permute-start | bytes 7077896 | tf_op jit(solution)/shard_map/ppermute | solution.py:23
  135.8 1398.4 %reduce-scatter.7.cloned.1.call-start = ((), (), s32[]{:S(2)}) async-start(), calls=%async_computation.9 | async-start | bytes 4718592 | tf_op jit(solution)/shard_map/reduce_scatter | solution.py:363
  313.4 344.5 %copy-start.37 = (f32[8,1,128]{2,1,0:T(1,128)}, f32[8,1,128]{2,1,0:T(1,128)S(1)}, u32[]{:S(2)}) copy-start(f32[8,1,128]{2,1,0:T(1,128)S(1)} %convert_element_type.351) | copy-start | bytes 12292
  332.4 440.4 %copy-start.33 = (f32[8,1,128]{2,1,0:T(1,128)}, f32[8,1,128]{2,1,0:T(1,128)S(1)}, u32[]{:S(2)}) copy-start(f32[8,1,128]{2,1,0:T(1,128)S(1)} %convert_element_type.350) | copy-start | bytes 12292
  341.2 181.1 %collective-permute-start.1 = (bf16[576,2048]{1,0:T(8,128)(2,1)}, bf16[576,2048]{1,0:T(8,128)(2,1)}, u32[]{:S(2)}, u32[]{:S(2)}) collective-permute-start(bf16[576,2048]{1,0:T(8,128)(2,1)} %pad_maximum_fusion.6), channel_id=1, source_target_pairs={{1,0},{2,1},{3,2},{4,3},{5,4},{6,5},{7,6},{9,8},{10,9},{11,10},{12... | collective-permute-start | bytes 7077896 | tf_op jit(solution)/shard_map/ppermute | solution.py:26
  342.5 179.8 %collective-permute-start = (bf16[576,2048]{1,0:T(8,128)(2,1)}, bf16[576,2048]{1,0:T(8,128)(2,1)}, u32[]{:S(2)}, u32[]{:S(2)}) collective-permute-start(bf16[576,2048]{1,0:T(8,128)(2,1)} %pad_maximum_fusion.6), channel_id=1, source_target_pairs={{0,1},{1,2},{2,3},{3,4},{4,5},{5,6},{6,7},{8,9},{9,10},{10,11},{11... | collective-permute-start | bytes 7077896 | tf_op jit(solution)/shard_map/ppermute | solution.py:23
  521.0 127.9 %copy-start.42 = (f32[576]{0:T(1024)}, f32[576]{0:T(1024)S(1)}, u32[]{:S(2)}) copy-start(f32[576]{0:T(1024)S(1)} %broadcast_multiply_fusion.8) | copy-start | bytes 6916
  554.9 89.7 %copy-start.76 = (f32[8,1,128]{2,1,0:T(1,128)S(1)}, f32[8,1,128]{2,1,0:T(1,128)}, u32[]{:S(2)}) copy-start(f32[8,1,128]{2,1,0:T(1,128)} %convert_element_type.349) | copy-start | bytes 12292
  648.5 124.3 %copy-start.1 = (f32[576,1024]{1,0:T(8,128)}, f32[576,1024]{1,0:T(8,128)S(1)}, u32[]{:S(2)}) copy-start(f32[576,1024]{1,0:T(8,128)S(1)} %get-tuple-element.746) | copy-start | bytes 7077892
  648.5 124.3 %copy-start.31 = (f32[576]{0:T(1024)}, f32[576]{0:T(1024)S(1)}, u32[]{:S(2)}) copy-start(f32[576]{0:T(1024)S(1)} %broadcast_multiply_fusion.10) | copy-start | bytes 6916
  648.9 123.9 %copy-start.35 = (f32[576]{0:T(1024)}, f32[576]{0:T(1024)S(1)}, u32[]{:S(2)}) copy-start(f32[576]{0:T(1024)S(1)} %add_rsqrt_fusion.2) | copy-start | bytes 6916
  989.7 269.4 %collective-permute-start.6 = (bf16[576,2048]{1,0:T(8,128)(2,1)}, bf16[576,2048]{1,0:T(8,128)(2,1)}, u32[]{:S(2)}, u32[]{:S(2)}) collective-permute-start(bf16[576,2048]{1,0:T(8,128)(2,1)} %copy.145), channel_id=1, source_target_pairs={{0,1},{1,2},{2,3},{3,4},{4,5},{5,6},{6,7},{8,9},{9,10},{10,11},{11... | collective-permute-start | bytes 7077896 | tf_op jit(solution)/shard_map/ppermute | solution.py:23
  995.5 268.0 %collective-permute-start.7 = (bf16[576,2048]{1,0:T(8,128)(2,1)}, bf16[576,2048]{1,0:T(8,128)(2,1)}, u32[]{:S(2)}, u32[]{:S(2)}) collective-permute-start(bf16[576,2048]{1,0:T(8,128)(2,1)} %copy.146), channel_id=1, source_target_pairs={{1,0},{2,1},{3,2},{4,3},{5,4},{6,5},{7,6},{9,8},{10,9},{11,10},{12... | collective-permute-start | bytes 7077896 | tf_op jit(solution)/shard_map/ppermute | solution.py:26
  1015.0 609.4 %reduce-scatter.5.cloned.1.call-start = ((), (), s32[]{:S(2)}) async-start(), calls=%async_computation.8 | async-start | bytes 14155776 | tf_op jit(solution)/shard_map/reduce_scatter | solution.py:360
  1246.9 92.7 %collective-permute-start.4 = (bf16[576,2048]{1,0:T(8,128)(2,1)}, bf16[576,2048]{1,0:T(8,128)(2,1)}, u32[]{:S(2)}, u32[]{:S(2)}) collective-permute-start(bf16[576,2048]{1,0:T(8,128)(2,1)} %copy.136), channel_id=1, source_target_pairs={{0,1},{1,2},{2,3},{3,4},{4,5},{5,6},{6,7},{8,9},{9,10},{10,11},{11... | collective-permute-start | bytes 7077896 | tf_op jit(solution)/shard_map/ppermute | solution.py:23
  1257.4 86.5 %collective-permute-start.5 = (bf16[576,2048]{1,0:T(8,128)(2,1)}, bf16[576,2048]{1,0:T(8,128)(2,1)}, u32[]{:S(2)}, u32[]{:S(2)}) collective-permute-start(bf16[576,2048]{1,0:T(8,128)(2,1)} %copy.137), channel_id=1, source_target_pairs={{1,0},{2,1},{3,2},{4,3},{5,4},{6,5},{7,6},{9,8},{10,9},{11,10},{12... | collective-permute-start | bytes 7077896 | tf_op jit(solution)/shard_map/ppermute | solution.py:26
  1295.4 53.0 %copy-start = (bf16[576,2048]{0,1:T(8,128)(2,1)S(1)}, bf16[576,2048]{0,1:T(8,128)(2,1)}, u32[]{:S(2)}) copy-start(bf16[576,2048]{0,1:T(8,128)(2,1)} %get-tuple-element.711) | copy-start | bytes 7077892
  1417.7 489.9 %reduce-scatter.9.cloned.1.call-start = ((), (), s32[]{:S(2)}) async-start(), calls=%async_computation.10 | async-start | bytes 18874368 | tf_op jit(solution)/shard_map/reduce_scatter | solution.py:367
  1447.8 742.9 %reduce-scatter.11.cloned.1.call-start = ((), (), s32[]{:S(2)}) async-start(), calls=%async_computation.11 | async-start | bytes 18874368 | tf_op jit(solution)/shard_map/reduce_scatter | solution.py:369
  1476.3 785.8 %all-reduce.14.cloned.1.call-start = ((), (), s32[]{:S(2)}) async-start(), calls=%async_computation.12 | async-start | bytes 6291456 | tf_op jit(solution)/shard_map/psum | solution.py:378
  (77 other events, 799.0 us)
Sparse Core Ops, SparseCore 0:
  10.2 101.5 all-gather.13
  113.9 102.8 all-gather.15
  218.9 131.3 all-gather.17
  352.3 162.9 all-gather.19
  1015.1 115.5 reduce-scatter.6
  1417.8 206.5 reduce-scatter.4
  1628.2 279.3 reduce-scatter.8
  1911.3 279.3 reduce-scatter.10
  2194.4 67.6 all-reduce.13
where the time goes:
time: 2300 us; the launch traced here: 2280 us
  matrix products  781 us (34%)
  waiting for transfers between devices  735 us (32%)
  blocking collectives  332 us (14%)
  local copies, waits for them, and re-layouts  226 us (10%)
  other arithmetic  157 us (7%)
  starting transfers between devices  27.8 us (1%)
    dot_general x104, matrix products, product_right(): lax.dot_general(left, right, (((1,), (1,)), ((), ())), preferred_element_...  321 us
    reduce_scatter x1, waiting for transfers between devices, body(): lax.psum_scatter(weight_grads[9], 'fsdp', scatter_dimension=0, tiled=True)  281 us
    reduce_scatter x1, waiting for transfers between devices, body(): lax.psum_scatter(weight_grads[11], 'fsdp', scatter_dimension=0, tiled=True)  280 us
    dot_general x72, matrix products, product(): return jnp.dot(left, right, preferred_element_type=jnp.float32)  242 us
    dot_general x72, matrix products, product_left(): lax.dot_general(left, right, (((0,), (0,)), ((), ())), preferred_element_...  218 us
    all_gather x1, blocking collectives, body(): lax.all_gather(shards[6], 'fsdp', axis=0, tiled=True)  132 us
    reduce_scatter x1, waiting for transfers between devices, body(): lax.psum_scatter(weight_grads[2], 'fsdp', scatter_dimension=0, tiled=True)  88.4 us
    unnamed x201, local copies, waits for them, and re-layouts  53.4 us
  transfers between devices with their start and end apart: 17, of which 6 were waited for; matrix products, arithmetic and copies ran while one was open for 38% of the time, Pallas kernels for 0%

commit v1 on v0

v1 whole, which is shorter than its diff:
```python
import jax
import jax.numpy as jnp
from jax import lax
from jax.experimental import pallas as pl
from jax.experimental.pallas import tpu as pltpu
from jax.sharding import PartitionSpec as P

D = 1024
HD = 64
IMG = 577


epsilon = 1e-06
masked_score = -1e30


def product(left, right):
    return jnp.dot(left, right, preferred_element_type=jnp.float32)


def product_left(left, right):
    return lax.dot_general(
        left, right, (((0,), (0,)), ((), ())), preferred_element_type=jnp.float32
    )


def product_right(left, right):
    return lax.dot_general(
        left, right, (((1,), (1,)), ((), ())), preferred_element_type=jnp.float32
    )


def norm_stats(values):
    centre = values - jnp.mean(values, axis=-1, keepdims=True)
    spread = jnp.mean(centre * centre, axis=-1, keepdims=True)
    factor = lax.rsqrt(spread + epsilon)
    return (centre * factor, factor)


def norm_back(grad_normed, normed, factor):
    return factor * (
        grad_normed
        - jnp.mean(grad_normed, axis=-1, keepdims=True)
        - normed * jnp.mean(grad_normed * normed, axis=-1, keepdims=True)
    )


QT = 192
KT = 192
PAIR = 128


def stacked_pair(rows):
    low = lax.broadcasted_iota(jnp.int32, rows.shape, 1) < HD
    zero = jnp.zeros_like(rows)
    return jnp.concatenate([jnp.where(low, rows, zero), jnp.where(low, zero, rows)], axis=0)


def merged_pair(columns):
    rows = columns.T
    half = rows.shape[0] // 2
    low = lax.broadcasted_iota(jnp.int32, (half, PAIR), 1) < HD
    return jnp.where(low, rows[:half], rows[half:])


def contract(left, right, left_dim, right_dim):
    return lax.dot_general(
        left,
        right,
        (((left_dim,), (right_dim,)), ((), ())),
        preferred_element_type=jnp.float32,
    )


def load_window(parts, window):
    rows = parts[0].shape[0]
    for index, part in enumerate(parts):
        window[index * rows : (index + 1) * rows, :] = part[...]


def tile_scores(key_rows, query_stack, key_label, query_label):
    scores = contract(key_rows, query_stack, 1, 1)
    wide = jnp.concatenate([key_label] * (query_stack.shape[0] // PAIR), axis=1)
    return jnp.where(wide == query_label, scores, masked_score)


def attend_forward_kernel(
    bounds,
    query,
    key_low,
    key_own,
    key_high,
    value_low,
    value_own,
    value_high,
    key_labels,
    query_labels,
    mixed,
    log_totals,
    keys,
    values,
):
    load_window((key_low, key_own, key_high), keys)
    load_window((value_low, value_own, value_high), values)
    for tile in range(query.shape[0] // QT):
        rows = slice(tile * QT, (tile + 1) * QT)
        query_stack = stacked_pair(query[rows, :] * jnp.bfloat16(HD**-0.5))
        query_label = query_labels[tile]
        width = 2 * QT

        def step(index, carry):
            largest, total, gathered = carry
            place = pl.ds(pl.multiple_of(index * KT, KT), KT)
            scores = tile_scores(keys[place, :], query_stack, key_labels[place, :], query_label)
            raised_to = jnp.maximum(largest, jnp.max(scores, axis=0, keepdims=True))
            raised = jnp.exp(scores - raised_to)
            fade = jnp.exp(largest - raised_to)
            total = total * fade + jnp.sum(raised, axis=0, keepdims=True)
            gathered = gathered * fade + contract(
                values[place, :], raised.astype(jnp.bfloat16), 0, 0
            )
            return (raised_to, total, gathered)

        largest, total, gathered = lax.fori_loop(
            bounds[2 * tile],
            bounds[2 * tile + 1],
            step,
            (
                jnp.full((1, width), masked_score, jnp.float32),
                jnp.zeros((1, width), jnp.float32),
                jnp.zeros((PAIR, width), jnp.float32),
            ),
        )
        mixed[rows, :] = merged_pair(gathered / total).astype(jnp.bfloat16)
        log_totals[0, tile] = largest + jnp.log(total)


def attend_backward_kernel(
    bounds,
    query,
    key_low,
    key_own,
    key_high,
    value_low,
    value_own,
    value_high,
    key_labels,
    query_labels,
    mixed,
    log_totals,
    grad_mixed,
    grad_query,
    grad_low,
    grad_own,
    grad_high,
    keys,
    values,
    grad_keys,
    grad_values,
):
    load_window((key_low, key_own, key_high), keys)
    load_window((value_low, value_own, value_high), values)
    grad_keys[...] = jnp.zeros_like(grad_keys)
    grad_values[...] = jnp.zeros_like(grad_values)
    for tile in range(query.shape[0] // QT):
        rows = slice(tile * QT, (tile + 1) * QT)
        query_stack = stacked_pair(query[rows, :] * jnp.bfloat16(HD**-0.5))
        grad_rows = grad_mixed[rows, :]
        grad_stack = stacked_pair(grad_rows)
        inner = grad_rows.astype(jnp.float32) * mixed[rows, :].astype(jnp.float32)
        row_inner = jnp.sum(stacked_pair(inner).T, axis=0, keepdims=True)
        query_label = query_labels[tile]
        log_total = log_totals[0, tile]

        def step(index, grad_columns):
            place = pl.ds(pl.multiple_of(index * KT, KT), KT)
            key_rows = keys[place, :]
            scores = tile_scores(key_rows, query_stack, key_labels[place, :], query_label)
            attention = jnp.exp(scores - log_total)
            grad_probs = contract(values[place, :], grad_stack, 1, 1)
            grad_scores = (attention * (grad_probs - row_inner)).astype(jnp.bfloat16)
            grad_keys[place, :] += contract(grad_scores, query_stack, 1, 0)
            grad_values[place, :] += contract(attention.astype(jnp.bfloat16), grad_stack, 1, 0)
            return grad_columns + contract(key_rows, grad_scores, 0, 0)

        grad_columns = lax.fori_loop(
            bounds[2 * tile],
            bounds[2 * tile + 1],
            step,
            jnp.zeros((PAIR, 2 * QT), jnp.float32),
        )
        grad_query[rows, :] = (merged_pair(grad_columns) * HD**-0.5).astype(jnp.bfloat16)
    shard_rows = query.shape[0]
    for slot, source in ((0, grad_keys), (1, grad_values)):
        grad_low[slot] = source[:shard_rows, :].astype(jnp.bfloat16)
        grad_own[slot] = source[shard_rows : 2 * shard_rows, :]
        grad_high[slot] = source[2 * shard_rows :, :].astype(jnp.bfloat16)


def attend_specs(shard_rows):
    tiles = shard_rows // QT
    column = pl.BlockSpec((shard_rows, PAIR), lambda pair, bounds: (0, pair))
    value = pl.BlockSpec((shard_rows, PAIR), lambda pair, bounds: (0, D // PAIR + pair))
    both = pl.BlockSpec((2, shard_rows, PAIR), lambda pair, bounds: (0, 0, pair))
    key_label = pl.BlockSpec((3 * shard_rows, PAIR), lambda pair, bounds: (0, 0))
    query_label = pl.BlockSpec((tiles, 1, 2 * QT), lambda pair, bounds: (0, 0, 0))
    log_total = pl.BlockSpec((1, tiles, 1, 2 * QT), lambda pair, bounds: (pair, 0, 0, 0))
    operands = [column] * 4 + [value] * 3 + [key_label, query_label]
    return column, both, log_total, operands


def attend_forward(bounds, query, low, own, high, key_labels, query_labels):
    shard_rows = query.shape[0]
    tiles = shard_rows // QT
    pairs = D // PAIR
    column, both, log_total, operands = attend_specs(shard_rows)
    window = pltpu.VMEM((3 * shard_rows, PAIR), jnp.bfloat16)
    pairs_seen = 2 * D * shard_rows * IMG * 2
    return pl.pallas_call(
        attend_forward_kernel,
        grid_spec=pltpu.PrefetchScalarGridSpec(
            num_scalar_prefetch=1,
            grid=(pairs,),
            in_specs=operands,
            out_specs=[column, log_total],
            scratch_shapes=[window, window],
        ),
        out_shape=[
            jax.ShapeDtypeStruct((shard_rows, D), jnp.bfloat16),
            jax.ShapeDtypeStruct((pairs, tiles, 1, 2 * QT), jnp.float32),
        ],
        cost_estimate=pl.CostEstimate(
            flops=4 * pairs_seen, bytes_accessed=20 * shard_rows * D, transcendentals=0
        ),
    )(bounds, query, low, own, high, low, own, high, key_labels, query_labels)


def attend_backward(
    bounds, query, low, own, high, key_labels, query_labels, mixed, log_totals, grad_mixed
):
    shard_rows = query.shape[0]
    column, both, log_total, operands = attend_specs(shard_rows)
    window = pltpu.VMEM((3 * shard_rows, PAIR), jnp.bfloat16)
    wide = pltpu.VMEM((3 * shard_rows, PAIR), jnp.float32)
    pairs_seen = 2 * D * shard_rows * IMG * 2
    rim = jax.ShapeDtypeStruct((2, shard_rows, D), jnp.bfloat16)
    return pl.pallas_call(
        attend_backward_kernel,
        grid_spec=pltpu.PrefetchScalarGridSpec(
            num_scalar_prefetch=1,
            grid=(D // PAIR,),
            in_specs=operands + [column, log_total, column],
            out_specs=[column, both, both, both],
            scratch_shapes=[window, window, wide, wide],
        ),
        out_shape=[
            jax.ShapeDtypeStruct((shard_rows, D), jnp.bfloat16),
            rim,
            jax.ShapeDtypeStruct((2, shard_rows, D), jnp.float32),
            rim,
        ],
        cost_estimate=pl.CostEstimate(
            flops=8 * pairs_seen, bytes_accessed=40 * shard_rows * D, transcendentals=0
        ),
    )(
        bounds,
        query,
        low,
        own,
        high,
        low,
        own,
        high,
        key_labels,
        query_labels,
        mixed,
        log_totals,
        grad_mixed,
    )


def attend_plan(query_start, shard_rows, starts):
    places = query_start - shard_rows + jnp.arange(3 * shard_rows, dtype=jnp.int32)
    after = starts[None, :] <= places[:, None]
    inside = after & (places[:, None] < starts[None, :] + IMG)
    counted = jnp.sum(after.astype(jnp.int32), axis=1) - 1
    owned = jnp.any(inside, axis=1)
    labels = jnp.where(owned, counted, -(2**24) - places)
    image = jnp.sum(jnp.where(inside, starts[None, :], 0), axis=1)
    own = slice(shard_rows, 2 * shard_rows)
    base = query_start - shard_rows
    first = jnp.where(owned, image, places)[own].reshape(-1, QT)[:, 0] - base
    last = jnp.where(owned, image + IMG, places + 1)[own].reshape(-1, QT)[:, -1] - base
    low = jnp.maximum(first, 0) // KT
    high = jnp.minimum((last + KT - 1) // KT, 3 * shard_rows // KT)
    bounds = jnp.stack([low, high], axis=1).reshape(-1).astype(jnp.int32)
    key_labels = jnp.broadcast_to(labels[:, None], (3 * shard_rows, PAIR))
    tiles = labels[own].reshape(-1, 1, QT)
    return bounds, key_labels, jnp.concatenate([tiles, tiles], axis=2)


def neighbours(low_going, high_going):
    count = lax.axis_size("fsdp")
    forward = [(i, i + 1) for i in range(count - 1)]
    backward = [(target, source) for source, target in forward]
    from_low = lax.ppermute(high_going, "fsdp", forward)
    from_high = lax.ppermute(low_going, "fsdp", backward)
    return from_low, from_high


def body(
    tokens,
    out_grad,
    image_starts,
    first_gain,
    first_shift,
    qkv_weight,
    query_bias,
    value_bias,
    out_weight,
    out_bias,
    second_gain,
    second_shift,
    up_weight,
    up_bias,
    down_weight,
    down_bias,
):
    micro_count, shard_rows, _ = tokens.shape
    query_start = lax.axis_index("fsdp") * shard_rows

    def gathered(shard):
        return lax.all_gather(shard, "fsdp", axis=0, tiled=True)

    small = jnp.concatenate(
        [
            jnp.stack(
                [
                    first_gain,
                    first_shift,
                    query_bias,
                    value_bias,
                    out_bias,
                    second_gain,
                    second_shift,
                    down_bias,
                ]
            ).reshape(-1),
            up_bias,
        ]
    )
    count = lax.axis_size("fsdp")
    small = gathered(small).reshape(count, -1).astype(jnp.float32)
    part = D // count
    (
        first_gain,
        first_shift,
        query_bias,
        value_bias,
        out_bias,
        second_gain,
        second_shift,
        down_bias,
    ) = [small[:, i * part : (i + 1) * part].reshape(-1) for i in range(8)]
    up_bias = small[:, 8 * part :].reshape(-1)
    qkv_weight = gathered(qkv_weight)
    out_weight = gathered(out_weight)
    up_weight = gathered(up_weight)
    down_weight = gathered(down_weight)

    plans = [
        attend_plan(query_start, shard_rows, image_starts[micro, 0])
        for micro in range(micro_count)
    ]
    inputs = tokens.reshape(-1, D).astype(jnp.float32)
    normed_one, factor_one = norm_stats(inputs)
    first_in = (normed_one * first_gain + first_shift).astype(jnp.bfloat16)
    joined_bias = jnp.concatenate([query_bias, jnp.zeros_like(query_bias), value_bias])
    joined = (product(first_in, qkv_weight) + joined_bias).astype(jnp.bfloat16)
    operands = []
    mixed_parts = []
    for micro in range(micro_count):
        rows = joined[micro * shard_rows : (micro + 1) * shard_rows]
        own = rows[:, D:]
        low, high = neighbours(own, own)
        bounds, key_labels, query_labels = plans[micro]
        operand = (bounds, rows[:, :D], low, own, high, key_labels, query_labels)
        mixed, log_totals = attend_forward(*operand)
        operands.append(operand + (mixed, log_totals))
        mixed_parts.append(mixed)
    mixed_rows = jnp.concatenate(mixed_parts, axis=0)
    middle = inputs + product(mixed_rows, out_weight) + out_bias
    normed_two, factor_two = norm_stats(middle)
    second_in = (normed_two * second_gain + second_shift).astype(jnp.bfloat16)
    hidden = product(second_in, up_weight) + up_bias
    phi = 0.5 * (1.0 + lax.erf(hidden * (2.0**-0.5)))
    active = (hidden * phi).astype(jnp.bfloat16)
    slope = phi + hidden * jnp.exp(-0.5 * hidden * hidden) * ((2.0 * jnp.pi) ** -0.5)
    layer_out = (middle + product(active, down_weight) + down_bias).astype(jnp.bfloat16)

    cotangent = out_grad.reshape(-1, D)
    grad_out = cotangent.astype(jnp.float32)
    down_grad = product_left(active, cotangent)
    down_bias_grad = jnp.sum(grad_out, axis=0)
    grad_hidden = (product_right(cotangent, down_weight) * slope).astype(jnp.bfloat16)
    up_grad = product_left(second_in, grad_hidden)
    up_bias_grad = jnp.sum(grad_hidden.astype(jnp.float32), axis=0)
    grad_second = product_right(grad_hidden, up_weight)
    second_gain_grad = jnp.sum(grad_second * normed_two, axis=0)
    second_shift_grad = jnp.sum(grad_second, axis=0)
    grad_middle = grad_out + norm_back(grad_second * second_gain, normed_two, factor_two)
    grad_branch = grad_middle.astype(jnp.bfloat16)
    out_weight_grad = product_left(mixed_rows, grad_branch)
    out_bias_grad = jnp.sum(grad_branch.astype(jnp.float32), axis=0)
    grad_mixed = product_right(grad_branch, out_weight).astype(jnp.bfloat16)
    grad_queries = []
    grad_pairs = []
    for micro in range(micro_count):
        grad_query, grad_low, grad_own, grad_high = attend_backward(
            *operands[micro], grad_mixed[micro * shard_rows : (micro + 1) * shard_rows]
        )
        from_low, from_high = neighbours(grad_low, grad_high)
        grad_pair = (
            grad_own + from_low.astype(jnp.float32) + from_high.astype(jnp.float32)
        ).astype(jnp.bfloat16)
        grad_queries.append(grad_query)
        grad_pairs.append(grad_pair)
    grad_joined = jnp.concatenate(
        [
            jnp.concatenate([query_part, pair[0], pair[1]], axis=1)
            for query_part, pair in zip(grad_queries, grad_pairs)
        ],
        axis=0,
    )
    qkv_grad = product_left(first_in, grad_joined)
    joined_sums = jnp.sum(grad_joined.astype(jnp.float32), axis=0)
    grad_first = product_right(grad_joined, qkv_weight)
    first_gain_grad = jnp.sum(grad_first * normed_one, axis=0)
    first_shift_grad = jnp.sum(grad_first, axis=0)
    tokens_grad = (
        grad_middle + norm_back(grad_first * first_gain, normed_one, factor_one)
    ).astype(jnp.bfloat16)

    def reduced(grad):
        return lax.psum_scatter(
            grad.astype(jnp.bfloat16), "fsdp", scatter_dimension=0, tiled=True
        )

    def replicas(grad):
        return lax.psum(grad, "rep").astype(jnp.float32)

    small_grads = [
        first_gain_grad,
        first_shift_grad,
        joined_sums[:D],
        joined_sums[2 * D :],
        out_bias_grad,
        second_gain_grad,
        second_shift_grad,
        down_bias_grad,
        up_bias_grad,
    ]
    packed = jnp.concatenate([grad.reshape(count, -1) for grad in small_grads], axis=1)
    packed = lax.psum(packed, ("rep", "fsdp"))
    packed = lax.dynamic_index_in_dim(packed, lax.axis_index("fsdp"), 0, keepdims=False)
    smalls = [packed[i * part : (i + 1) * part] for i in range(8)] + [packed[8 * part :]]
    down_grad = replicas(reduced(down_grad))
    up_grad = replicas(reduced(up_grad))
    out_weight_grad = replicas(reduced(out_weight_grad))
    qkv_grad = replicas(reduced(qkv_grad))
    return (
        layer_out.reshape(tokens.shape),
        tokens_grad.reshape(tokens.shape),
        smalls[0],
        smalls[1],
        qkv_grad,
        smalls[2],
        smalls[3],
        out_weight_grad,
        smalls[4],
        smalls[5],
        smalls[6],
        up_grad,
        smalls[8],
        down_grad,
        smalls[7],
    )


def solution(mesh):
    placed = (
        P(None, ("rep", "fsdp"), None),
        P(None, ("rep", "fsdp"), None),
        P(None, "rep", None),
        P("fsdp"),
        P("fsdp"),
        P("fsdp", None),
        P("fsdp"),
        P("fsdp"),
        P("fsdp", None),
        P("fsdp"),
        P("fsdp"),
        P("fsdp"),
        P("fsdp", None),
        P("fsdp"),
        P("fsdp", None),
        P("fsdp"),
    )
    return jax.shard_map(
        body,
        mesh=mesh,
        in_specs=placed,
        out_specs=(
            P(None, ("rep", "fsdp"), None),
            P(None, ("rep", "fsdp"), None),
            P("fsdp"),
            P("fsdp"),
            P("fsdp", None),
            P("fsdp"),
            P("fsdp"),
            P("fsdp", None),
            P("fsdp"),
            P("fsdp"),
            P("fsdp"),
            P("fsdp", None),
            P("fsdp"),
            P("fsdp", None),
            P("fsdp"),
        ),
        check_vma=False,
    )
```

time: 2300 us -> 1460 us (0.63)
  matrix products: 781 us -> 163 us
  blocking collectives: 332 us -> 86.6 us
  Pallas kernels: 0 us -> 210 us
  local copies, waits for them, and re-layouts: 226 us -> 27.2 us
  waiting for transfers between devices: 735 us -> 849 us
  other arithmetic: 157 us -> 78.8 us
    reduce_scatter x4, waiting for transfers between devices: 650 us -> 308 us  [reduced(): lax.psum_scatter(grad.astype(jnp.bfloat16), 'fsdp', scatter_dimension=0,...]
    ppermute x8, waiting for transfers between devices: 44.3 us -> 325 us  [the longest x4 325 us: neighbours(): from_low = lax.ppermute(high_going, 'fsdp', forward)]
    dot_general x104 -> x4, matrix products: 321 us -> 55 us  [product_right(): lax.dot_general(left, right, (((1,), (1,)), ((), ())), preferred_element_...]
    all_gather x9 -> x1, blocking collectives: 291 us -> 33.3 us  [gathered(): return lax.all_gather(shard, 'fsdp', axis=0, tiled=True)]
    pallas_call x0 -> x4, Pallas kernels: none -> 210 us  [the longest x2 110 us: attend_backward(): pl.pallas_call(attend_backward_kernel, grid_spec=pltpu.PrefetchScalarGrid...]
    dot_general x72 -> x4, matrix products: 242 us -> 52.4 us  [product(): return jnp.dot(left, right, preferred_element_type=jnp.float32)]
    dot_general x72 -> x4, matrix products: 218 us -> 56.1 us  [product_left(): lax.dot_general(left, right, (((0,), (0,)), ((), ())), preferred_element_...]
    all_gather x4, waiting for transfers between devices: 23.5 us -> 148 us  [gathered(): return lax.all_gather(shard, 'fsdp', axis=0, tiled=True)]
  transfers between devices with their start and end apart: 17 -> 17, of which waited for: 6 -> 10; matrix products, arithmetic and copies ran while one was open for 38% -> 14% of each run, Pallas kernels for 0% -> 11%
where the time goes in v1:
time: 1460 us; the launch traced here: 1450 us
  waiting for transfers between devices  849 us (58%)
  Pallas kernels  210 us (14%)
  matrix products  163 us (11%)
  blocking collectives  86.6 us (6%)
  other arithmetic  78.8 us (5%)
  local copies, waits for them, and re-layouts  27.2 us (2%)
  starting transfers between devices  22.1 us (2%)
  between operations  14.8 us (1%)
    ppermute x4, waiting for transfers between devices, neighbours(): from_low = lax.ppermute(high_going, 'fsdp', forward)  325 us
    reduce_scatter x4, waiting for transfers between devices, reduced(): lax.psum_scatter(grad.astype(jnp.bfloat16), 'fsdp', scatter_dimension=0,...  308 us
    all_gather x4, waiting for transfers between devices, gathered(): return lax.all_gather(shard, 'fsdp', axis=0, tiled=True)  148 us
    pallas_call x2, Pallas kernels, attend_backward(): pl.pallas_call(attend_backward_kernel, grid_spec=pltpu.PrefetchScalarGrid...  110 us
    pallas_call x2, Pallas kernels, attend_forward(): pl.pallas_call(attend_forward_kernel, grid_spec=pltpu.PrefetchScalarGridS...  100 us
    psum x1, waiting for transfers between devices, replicas(): return lax.psum(grad, 'rep').astype(jnp.float32)  64.5 us
    dot_general x4, matrix products, product_left(): lax.dot_general(left, right, (((0,), (0,)), ((), ())), preferred_element_...  56.1 us
    dot_general x4, matrix products, product_right(): lax.dot_general(left, right, (((1,), (1,)), ((), ())), preferred_element_...  55 us
  transfers between devices with their start and end apart: 17, of which 10 were waited for; matrix products, arithmetic and copies ran while one was open for 14% of the time, Pallas kernels for 11%

profile of v1, /device:TPU:0, one launch (start us, length us, event | category | flops | bytes accessed | tf_op | source)
XLA Modules:
  0.0 1451.8 jit_solution(10586287340178048727)
XLA Ops:
  11.5 33.3 %all-gather = bf16[8,1,1536]{2,1,0:T(2,128)(2,1)S(1)} all-gather(bf16[1,1,1536]{2,1,0:T(2,128)(2,1)S(1)} %reshape.318), channel_id=1, replica_groups=mesh['rep'=4,'fsdp'=8] {'fsdp'}, dimensions={0}, use_global_device_ids=true | all-gather | bytes 27648 | tf_op jit(solution)/shard_map/all_gather | solution.py:333
  49.7 62.3 %all-gather.6.cloned.1.call-done = bf16[1024,3072]{1,0:T(8,128)(2,1)} async-done(((bf16[128,3072]{1,0:T(8,128)(2,1)}), bf16[1024,3072]{1,0:T(8,128)(2,1)}) %all-gather.6.cloned.1.call-update) | async-done | bytes 6291472 | tf_op jit(solution)/shard_map/all_gather | solution.py:333
  112.0 10.3 add_convert_fusion
  127.9 3.9 collective-permute-start
  133.4 6.0 collective-permute-start.2
  147.5 158.4 %collective-permute-done.key_low.value_low = bf16[576,2048]{1,0:T(8,128)(2,1)} collective-permute-done((bf16[576,2048]{1,0:T(8,128)(2,1)}, bf16[576,2048]{1,0:T(8,128)(2,1)}, u32[]{:S(2)}, u32[]{:S(2)}) %collective-permute-start) | collective-permute-done | bytes 2359328 | tf_op jit(solution)/shard_map/ppermute | solution.py:306
  307.1 50.1 %shard_map.271 = (bf16[576,1024]{1,0:T(8,128)(2,1)}, f32[8,3,1,384]{3,2,1,0:T(1,128)}) custom-call(s32[6]{0:T(128)} %reshape.301.bounds, bf16[576,1024]{1,0:T(8,128)(2,1)} %get-tuple-element.66.query, bf16[576,2048]{1,0:T(8,128)(2,1)} %collective-permute-done.key_low.value_low, bf16[576,2048]{1,0:T(8,128)(2,1)} %get-tuple-element.64.key_own.value_own, ...), custom_call_target="tpu_custom_call" | custom-call | flops 5445255168 | bytes 11796480 | tf_op jit(solution)/shard_map/pallas_call | solution.py:219
  359.6 26.5 %collective-permute-done.2.key_low.value_low = bf16[576,2048]{1,0:T(8,128)(2,1)} collective-permute-done((bf16[576,2048]{1,0:T(8,128)(2,1)}, bf16[576,2048]{1,0:T(8,128)(2,1)}, u32[]{:S(2)}, u32[]{:S(2)}) %collective-permute-start.2) | collective-permute-done | bytes 2359328 | tf_op jit(solution)/shard_map/ppermute | solution.py:306
  387.3 49.9 %shard_map.272 = (bf16[576,1024]{1,0:T(8,128)(2,1)}, f32[8,3,1,384]{3,2,1,0:T(1,128)}) custom-call(s32[6]{0:T(128)} %reshape.305.bounds, bf16[576,1024]{1,0:T(8,128)(2,1)} %get-tuple-element.65.query, bf16[576,2048]{1,0:T(8,128)(2,1)} %collective-permute-done.2.key_low.value_low, bf16[576,2048]{1,0:T(8,128)(2,1)} %get-tuple-element.63.key_own.value_own, ...), custom_call_target="tpu_custom_call" | custom-call | flops 5445255168 | bytes 11796480 | tf_op jit(solution)/shard_map/pallas_call | solution.py:219
  439.7 5.3 fusion.46
  447.8 19.7 %multiply_convert_fusion = (bf16[1152,4096]{1,0:T(8,128)(2,1)}, f32[1152,4096]{1,0:T(8,128)}) fusion(f32[4096]{0:T(1024)S(1)} %bitcast.149, bf16[1024,4096]{1,0:T(8,128)(2,1)} %all-gather.10.cloned.1.call-done, f32[1152,1024]{1,0:T(8,128)} %copy-done.2, f32[1024]{0:T(1024)S(1)} %get-tuple-element.82, f32[1024]{0:T(1024)S(1)} %get-tuple-element.83, ...), kind=kOutput, calls=%fused_computation.7 | convolution fusion | flops 9697886208 | bytes 41452544 | tf_op jit(solution)/shard_map/dot_general | solution.py:18
  467.4 85.9 %all-gather.12.cloned.1.call-done = bf16[4096,1024]{1,0:T(8,128)(2,1)} async-done(((bf16[512,1024]{1,0:T(8,128)(2,1)}), bf16[4096,1024]{1,0:T(8,128)(2,1)}) %all-gather.12.cloned.1.call-update) | async-done | bytes 8388624 | tf_op jit(solution)/shard_map/all_gather | solution.py:333
  553.3 20.6 %convert_reduce_fusion = (f32[4096]{0:T(1024)S(1)}, bf16[1152,4096]{1,0:T(8,128)(2,1)}) fusion(f32[1152,4096]{1,0:T(8,128)} %get-tuple-element.108, bf16[1152,1024]{1,0:T(8,128)(2,1)S(1)} %bitcast.142, bf16[4096,1024]{1,0:T(8,128)(2,1)} %all-gather.12.cloned.1.call-done), kind=kOutput, calls=%fused_computation.6 | convolution fusion | flops 9720295424 | bytes 39075840 | tf_op jit(solution)/shard_map/dot_general | solution.py:28
  574.0 17.0 %multiply_reduce_fusion = (f32[1024]{0:T(1024)}, f32[1152]{0:T(1024)S(1)}, f32[1152]{0:T(1024)S(1)}, f32[1024]{0:T(1024)}, f32[1152,1024]{1,0:T(8,128)S(1)}) fusion(f32[1152,1024]{1,0:T(8,128)S(1)} %bitcast.141, f32[1152]{0:T(1024)S(1)} %add_rsqrt_fusion, f32[1152]{0:T(1024)S(1)} %broadcast_multiply_fusion.4, f32[1024]{0:T(1024)S(1)} %get-tuple-element.83, ...), kind=kOutput, calls=%fused_computation.38 | convolution fusion | flops 9674289152 | bytes 27293696 | tf_op jit(solution)/shard_map/dot_general | solution.py:28
  597.7 55.0 %shard_map.273 = (bf16[576,1024]{1,0:T(8,128)(2,1)}, bf16[2,576,1024]{2,1,0:T(8,128)(2,1)}, f32[2,576,1024]{2,1,0:T(8,128)}, bf16[2,576,1024]{2,1,0:T(8,128)(2,1)}) custom-call(s32[6]{0:T(128)} %reshape.301.bounds, bf16[576,1024]{1,0:T(8,128)(2,1)} %get-tuple-element.66.query, bf16[576,2048]{1,0:T(8,128)(2,1)} %collective-permute-done.key_low.value_low, ...), custom_call_target="tpu_custom_call" | custom-call | flops 10890510336 | bytes 23592960 | tf_op jit(solution)/shard_map/pallas_call | solution.py:247
  657.9 55.1 %shard_map.274 = (bf16[576,1024]{1,0:T(8,128)(2,1)}, bf16[2,576,1024]{2,1,0:T(8,128)(2,1)}, f32[2,576,1024]{2,1,0:T(8,128)}, bf16[2,576,1024]{2,1,0:T(8,128)(2,1)}) custom-call(s32[6]{0:T(128)} %reshape.305.bounds, bf16[576,1024]{1,0:T(8,128)(2,1)} %get-tuple-element.65.query, bf16[576,2048]{1,0:T(8,128)(2,1)} %collective-permute-done.2.key_low.value_low, ...), custom_call_target="tpu_custom_call" | custom-call | flops 10890510336 | bytes 23592960 | tf_op jit(solution)/shard_map/pallas_call | solution.py:247
  717.1 7.3 convolution_convert_fusion.4
  724.5 92.3 %collective-permute-done.4 = bf16[2,576,1024]{2,1,0:T(8,128)(2,1)} collective-permute-done((bf16[2,576,1024]{2,1,0:T(8,128)(2,1)}, bf16[2,576,1024]{2,1,0:T(8,128)(2,1)}, u32[]{:S(2)}, u32[]{:S(2)}) %collective-permute-start.4) | collective-permute-done | bytes 2359328 | tf_op jit(solution)/shard_map/ppermute | solution.py:306
  816.7 5.3 add_convert_fusion.2
  822.3 47.9 %collective-permute-done.6 = bf16[2,576,1024]{2,1,0:T(8,128)(2,1)} collective-permute-done((bf16[2,576,1024]{2,1,0:T(8,128)(2,1)}, bf16[2,576,1024]{2,1,0:T(8,128)(2,1)}, u32[]{:S(2)}, u32[]{:S(2)}) %collective-permute-start.6) | collective-permute-done | bytes 2359328 | tf_op jit(solution)/shard_map/ppermute | solution.py:306
  875.5 47.2 %convert_reduce_fusion.1 = (f32[3072]{0:T(1024)S(1)}, bf16[1152,3072]{1,0:T(8,128)(2,1)}) fusion(bf16[576,1024]{1,0:T(8,128)(2,1)S(1)} %get-tuple-element.72, bf16[576,1024]{1,0:T(8,128)(2,1)S(1)} %get-tuple-element.71, bf16[576,1024]{1,0:T(8,128)(2,1)S(1)} %copy-done.8, bf16[576,1024]{1,0:T(8,128)(2,1)S(1)} %get-tuple-element.68, ...), kind=kLoop, calls=%fused_computation.11 | loop fusion | flops 49542144 | bytes 14168064 | tf_op jit(solution)/shard_map/reduce_sum | solution.py:436
  922.7 13.3 convolution_convert_fusion.2
  936.1 17.9 %convolution_convert_fusion.1 = bf16[1024,4096]{1,0:T(8,128)(2,1)} fusion(bf16[1152,4096]{1,0:T(8,128)(2,1)} %get-tuple-element.112, f32[1152,1024]{1,0:T(8,128)} %copy-done.2, f32[1024]{0:T(1024)S(1)} %get-tuple-element.82, f32[1024]{0:T(1024)S(1)} %get-tuple-element.83, f32[1152]{0:T(1024)S(1)} %add_rsqrt_fusion, f32[1152]{0:T(1024)S(1)} %broadcast_multiply_fusion.4), kind=kOutput, calls=%fused_computation.14 | convolution fusion | flops 9673768960 | bytes 22561792 | tf_op jit(solution)/shard_map/dot_general | solution.py:22
  954.0 17.6 %convolution_convert_fusion = bf16[4096,1024]{1,0:T(8,128)(2,1)} fusion(bf16[1152,4096]{1,0:T(8,128)(2,1)} %get-tuple-element.107, bf16[1152,1024]{1,0:T(8,128)(2,1)S(1)} %bitcast.143), kind=kOutput, calls=%fused_computation.13 | convolution fusion | flops 9667870720 | bytes 20185088 | tf_op jit(solution)/shard_map/dot_general | solution.py:22
  972.3 17.1 %add_convert_fusion.3 = bf16[1152,1024]{1,0:T(8,128)(2,1)} fusion(f32[1152,1024]{1,0:T(8,128)} %copy-done.2, bf16[1152,4096]{1,0:T(8,128)(2,1)} %get-tuple-element.107, bf16[4096,1024]{1,0:T(8,128)(2,1)} %all-gather.12.cloned.1.call-done, f32[1024]{0:T(1024)S(1)} %copy-done.17), kind=kOutput, calls=%fused_computation.44 | convolution fusion | flops 9667215360 | bytes 24907776 | tf_op jit(solution)/shard_map/dot_general | solution.py:18
  989.5 14.4 fusion.19
  1004.0 53.2 %psum.35 = f32[8,1536]{1,0:T(8,128)S(1)} all-reduce(f32[8,1536]{1,0:T(8,128)S(1)} %constant_dynamic-update-slice_fusion.2), channel_id=1, replica_groups=mesh['rep'=4,'fsdp'=8] {'rep','fsdp'}, use_global_device_ids=true, to_apply=%region_22.23 | all-reduce | flops 12288 | bytes 98304 | tf_op jit(solution)/shard_map/psum | solution.py:464
  1058.5 7.9 reduce-scatter.5.cloned.1.call-done
  1066.5 150.1 %reduce-scatter.9.cloned.1.call-done = bf16[128,4096]{1,0:T(8,128)(2,1)} async-done(((bf16[1024,4096]{1,0:T(8,128)(2,1)}), bf16[128,4096]{1,0:T(8,128)(2,1)}) %reduce-scatter.9.cloned.1.call-update) | async-done | bytes 1048592 | tf_op jit(solution)/shard_map/reduce_scatter | solution.py:445
  1216.6 150.2 %reduce-scatter.11.cloned.1.call-done = bf16[512,1024]{1,0:T(8,128)(2,1)} async-done(((bf16[4096,1024]{1,0:T(8,128)(2,1)}), bf16[512,1024]{1,0:T(8,128)(2,1)}) %reduce-scatter.11.cloned.1.call-update) | async-done | bytes 1048592 | tf_op jit(solution)/shard_map/reduce_scatter | solution.py:445
  1366.8 5.6 fusion.18
  1372.5 64.5 %all-reduce.3.cloned.1.call-done = (bf16[128,3072]{1,0:T(8,128)(2,1)}, bf16[128,1024]{1,0:T(8,128)(2,1)}, bf16[128,4096]{1,0:T(8,128)(2,1)}, bf16[512,1024]{1,0:T(8,128)(2,1)}) async-done(((bf16[128,3072]{1,0:T(8,128)(2,1)}, bf16[128,1024]{1,0:T(8,128)(2,1)}, bf16[128,4096]{1,0:T(8,128)(2,1)}, bf16[512,1024]{1,0:T(8,128)(2,1)}), (bf16[128,3072]{1,0:T(8,128)(2,1)}, bf16[128,1024]{1,0:T(8,128)(2,1)}, ...) | async-done | bytes 3145744 | tf_op jit(solution)/shard_map/psum | solution.py:450
  (161 shorter events, 65.6 us)
Async XLA Ops:
  7.2 37.7 %copy-start = (bf16[2,576,1024]{2,1,0:T(8,128)(2,1)S(1)}, bf16[2,576,1024]{2,1,0:T(8,128)(2,1)}, u32[]{:S(2)}) copy-start(bf16[2,576,1024]{2,1,0:T(8,128)(2,1)} %param.16) | copy-start | bytes 7077892
  7.2 39.6 %copy-start.20 = (s32[2,1,6]{2,1,0:T(1,128)S(1)}, s32[2,1,6]{2,1,0:T(1,128)}, u32[]{:S(2)}) copy-start(s32[2,1,6]{2,1,0:T(1,128)} %param.18) | copy-start | bytes 148
  7.2 104.8 %all-gather.6.cloned.1.call-start = ((), (), s32[]{:S(2)}) async-start(), calls=%async_computation.4 | async-start | bytes 7077888 | tf_op jit(solution)/shard_map/all_gather | solution.py:333
  7.9 431.7 %all-gather.8.cloned.1.call-start = ((), (), s32[]{:S(2)}) async-start(), calls=%async_computation.5 | async-start | bytes 2359296 | tf_op jit(solution)/shard_map/all_gather | solution.py:333
  8.7 439.0 %all-gather.10.cloned.1.call-start = ((), (), s32[]{:S(2)}) async-start(), calls=%async_computation.6 | async-start | bytes 9437184 | tf_op jit(solution)/shard_map/all_gather | solution.py:333
  9.4 543.9 %all-gather.12.cloned.1.call-start = ((), (), s32[]{:S(2)}) async-start(), calls=%async_computation.7 | async-start | bytes 9437184 | tf_op jit(solution)/shard_map/all_gather | solution.py:333
  10.0 1048.5 %reduce-scatter.7.cloned.1.call-start = ((), (), s32[]{:S(2)}) async-start(), calls=%async_computation.9 | async-start | bytes 2359296 | tf_op jit(solution)/shard_map/reduce_scatter | solution.py:445
  45.4 77.0 %copy-start.11 = (f32[1152]{0:T(1024)}, f32[1152]{0:T(1024)S(1)}, u32[]{:S(2)}) copy-start(f32[1152]{0:T(1024)S(1)} %div.51) | copy-start | bytes 13828
  46.2 76.2 %copy-start.13 = (f32[1152]{0:T(1024)}, f32[1152]{0:T(1024)S(1)}, u32[]{:S(2)}) copy-start(f32[1152]{0:T(1024)S(1)} %rsqrt.20) | copy-start | bytes 13828
  127.9 178.0 %collective-permute-start = (bf16[576,2048]{1,0:T(8,128)(2,1)}, bf16[576,2048]{1,0:T(8,128)(2,1)}, u32[]{:S(2)}, u32[]{:S(2)}) collective-permute-start(bf16[576,2048]{1,0:T(8,128)(2,1)} %get-tuple-element.64.key_own.value_own), channel_id=1, source_target_pairs={{0,1},{1,2},{2,3},{3,4},{4,5},{5,6},{6,7},{8,9},{9,10},{10,11},{11... | collective-permute-start | bytes 7077896 | tf_op jit(solution)/shard_map/ppermute | solution.py:306
  131.8 174.1 %collective-permute-start.1 = (bf16[576,2048]{1,0:T(8,128)(2,1)}, bf16[576,2048]{1,0:T(8,128)(2,1)}, u32[]{:S(2)}, u32[]{:S(2)}) collective-permute-start(bf16[576,2048]{1,0:T(8,128)(2,1)} %get-tuple-element.64.key_own.value_own), channel_id=1, source_target_pairs={{1,0},{2,1},{3,2},{4,3},{5,4},{6,5},{7,6},{9,8},{10,9},{11,10},{12... | collective-permute-start | bytes 7077896 | tf_op jit(solution)/shard_map/ppermute | solution.py:307
  133.4 252.6 %collective-permute-start.2 = (bf16[576,2048]{1,0:T(8,128)(2,1)}, bf16[576,2048]{1,0:T(8,128)(2,1)}, u32[]{:S(2)}, u32[]{:S(2)}) collective-permute-start(bf16[576,2048]{1,0:T(8,128)(2,1)} %get-tuple-element.63.key_own.value_own), channel_id=1, source_target_pairs={{0,1},{1,2},{2,3},{3,4},{4,5},{5,6},{6,7},{8,9},{9,10},{10,11},{11... | collective-permute-start | bytes 7077896 | tf_op jit(solution)/shard_map/ppermute | solution.py:306
  139.5 246.6 %collective-permute-start.3 = (bf16[576,2048]{1,0:T(8,128)(2,1)}, bf16[576,2048]{1,0:T(8,128)(2,1)}, u32[]{:S(2)}, u32[]{:S(2)}) collective-permute-start(bf16[576,2048]{1,0:T(8,128)(2,1)} %get-tuple-element.63.key_own.value_own), channel_id=1, source_target_pairs={{1,0},{2,1},{3,2},{4,3},{5,4},{6,5},{7,6},{9,8},{10,9},{11,10},{12... | collective-permute-start | bytes 7077896 | tf_op jit(solution)/shard_map/ppermute | solution.py:307
  447.7 105.6 %copy-start.4 = (bf16[2,576,1024]{2,1,0:T(8,128)(2,1)S(1)}, bf16[2,576,1024]{2,1,0:T(8,128)(2,1)}, u32[]{:S(2)}) copy-start(bf16[2,576,1024]{2,1,0:T(8,128)(2,1)} %param.17) | copy-start | bytes 7077892
  447.7 126.2 %slice-start = ((s8[4718592]{0:T(1024)(128)(4,1)}), s8[524288]{0:T(1024)(128)(4,1)S(1)}, s32[]{:S(2)}) async-start(s8[4718592]{0:T(1024)(128)(4,1)} %bitcast.140), calls=%async_computation.13 | async-start | bytes 1048576
  553.3 20.6 %slice-start.1 = ((s8[4718592]{0:T(1024)(128)(4,1)}), s8[4194304]{0:T(1024)(128)(4,1)S(1)}, s32[]{:S(2)}) async-start(s8[4718592]{0:T(1024)(128)(4,1)} %bitcast.140), calls=%async_computation.14 | async-start | bytes 8388608
  652.8 164.0 %collective-permute-start.4 = (bf16[2,576,1024]{2,1,0:T(8,128)(2,1)}, bf16[2,576,1024]{2,1,0:T(8,128)(2,1)}, u32[]{:S(2)}, u32[]{:S(2)}) collective-permute-start(bf16[2,576,1024]{2,1,0:T(8,128)(2,1)} %get-tuple-element.32), channel_id=1, source_target_pairs={{0,1},{1,2},{2,3},{3,4},{4,5},{5,6},{6,7},{8,9},{9,10},{10,11},{11... | collective-permute-start | bytes 7077896 | tf_op jit(solution)/shard_map/ppermute | solution.py:306
  656.6 160.1 %collective-permute-start.5 = (bf16[2,576,1024]{2,1,0:T(8,128)(2,1)}, bf16[2,576,1024]{2,1,0:T(8,128)(2,1)}, u32[]{:S(2)}, u32[]{:S(2)}) collective-permute-start(bf16[2,576,1024]{2,1,0:T(8,128)(2,1)} %get-tuple-element.33), channel_id=1, source_target_pairs={{1,0},{2,1},{3,2},{4,3},{5,4},{6,5},{7,6},{9,8},{10,9},{11,10},{12... | collective-permute-start | bytes 7077896 | tf_op jit(solution)/shard_map/ppermute | solution.py:307
  713.0 157.2 %collective-permute-start.6 = (bf16[2,576,1024]{2,1,0:T(8,128)(2,1)}, bf16[2,576,1024]{2,1,0:T(8,128)(2,1)}, u32[]{:S(2)}, u32[]{:S(2)}) collective-permute-start(bf16[2,576,1024]{2,1,0:T(8,128)(2,1)} %get-tuple-element.37), channel_id=1, source_target_pairs={{0,1},{1,2},{2,3},{3,4},{4,5},{5,6},{6,7},{8,9},{9,10},{10,11},{11... | collective-permute-start | bytes 7077896 | tf_op jit(solution)/shard_map/ppermute | solution.py:306
  715.8 154.4 %collective-permute-start.7 = (bf16[2,576,1024]{2,1,0:T(8,128)(2,1)}, bf16[2,576,1024]{2,1,0:T(8,128)(2,1)}, u32[]{:S(2)}, u32[]{:S(2)}) collective-permute-start(bf16[2,576,1024]{2,1,0:T(8,128)(2,1)} %get-tuple-element.38), channel_id=1, source_target_pairs={{1,0},{2,1},{3,2},{4,3},{5,4},{6,5},{7,6},{9,8},{10,9},{11,10},{12... | collective-permute-start | bytes 7077896 | tf_op jit(solution)/shard_map/ppermute | solution.py:307
  724.4 145.8 %slice-start.2 = ((s8[4718592]{0:T(1024)(128)(4,1)}), s8[524288]{0:T(1024)(128)(4,1)S(1)}, s32[]{:S(2)}) async-start(s8[4718592]{0:T(1024)(128)(4,1)} %bitcast.144), calls=%async_computation.15 | async-start | bytes 1048576
  724.4 342.1 %reduce-scatter.5.cloned.1.call-start = ((), (), s32[]{:S(2)}) async-start(), calls=%async_computation.8 | async-start | bytes 7077888 | tf_op jit(solution)/shard_map/reduce_scatter | solution.py:445
  816.7 53.4 %slice-start.3 = ((s8[4718592]{0:T(1024)(128)(4,1)}), s8[4194304]{0:T(1024)(128)(4,1)S(1)}, s32[]{:S(2)}) async-start(s8[4718592]{0:T(1024)(128)(4,1)} %bitcast.144), calls=%async_computation.16 | async-start | bytes 8388608
  875.5 47.2 %copy-start.6 = (bf16[1152,1024]{1,0:T(8,128)(2,1)S(1)}, bf16[1152,1024]{1,0:T(8,128)(2,1)}, u32[]{:S(2)}) copy-start(bf16[1152,1024]{1,0:T(8,128)(2,1)} %fusion.13) | copy-start | bytes 7077892
  936.0 280.5 %reduce-scatter.9.cloned.1.call-start = ((), (), s32[]{:S(2)}) async-start(), calls=%async_computation.10 | async-start | bytes 9437184 | tf_op jit(solution)/shard_map/reduce_scatter | solution.py:445
  954.0 412.8 %reduce-scatter.11.cloned.1.call-start = ((), (), s32[]{:S(2)}) async-start(), calls=%async_computation.11 | async-start | bytes 9437184 | tf_op jit(solution)/shard_map/reduce_scatter | solution.py:445
  971.7 465.3 %all-reduce.3.cloned.1.call-start = ((), (), s32[]{:S(2)}) async-start(), calls=%async_computation.12 | async-start | bytes 6291456 | tf_op jit(solution)/shard_map/psum | solution.py:450
  972.3 17.1 %copy-start.1 = (bf16[2,576,1024]{2,1,0:T(8,128)(2,1)S(1)}, bf16[2,576,1024]{2,1,0:T(8,128)(2,1)}, u32[]{:S(2)}) copy-start(bf16[2,576,1024]{2,1,0:T(8,128)(2,1)} %param.16) | copy-start | bytes 7077892
  972.3 17.1 %copy-start.12 = (f32[1152]{0:T(1024)S(1)}, f32[1152]{0:T(1024)}, u32[]{:S(2)}) copy-start(f32[1152]{0:T(1024)} %copy-done.11) | copy-start | bytes 13828
  972.3 17.1 %copy-start.14 = (f32[1152]{0:T(1024)S(1)}, f32[1152]{0:T(1024)}, u32[]{:S(2)}) copy-start(f32[1152]{0:T(1024)} %copy-done.13) | copy-start | bytes 13828
  972.3 17.1 %copy-start.16 = (f32[1024]{0:T(1024)S(1)}, f32[1024]{0:T(1024)}, u32[]{:S(2)}) copy-start(f32[1024]{0:T(1024)} %copy-done.15) | copy-start | bytes 12292
  989.5 14.5 copy-start.18
  (11 other events, 41.3 us)
Sparse Core Ops, SparseCore 0:
  10.2 101.8 all-gather.5
  114.2 152.2 all-gather.7
  268.6 160.3 all-gather.9
  431.0 122.2 all-gather.11
  724.5 133.1 reduce-scatter.6
  936.1 130.2 reduce-scatter.4
  1070.1 146.4 reduce-scatter.8
  1220.2 146.5 reduce-scatter.10
  1369.4 67.5 all-reduce.2
